TPU v7x, 512 devices: a whole 4x8x8 slice. The times are simulated.
512 devices in a mesh: pts: 128 (over z, y, core), ch: 4 (over x).
Axes of the slice: x: 4, y: 8, z: 8, core: 2. Of those that a mesh axis runs over, the one named last changes fastest.
Arguments:
- points_in: bfloat16 [65536, 256], P('pts'), may hold values from -6 to 6
- neighbor_offsets: int32 [65536, 16], P('pts'), may hold values from -128 to 128, as said below
- kernel_ids: int32 [65536, 16], P('pts'), may hold values from 0 to 26
- cluster_ids: int32 [65536], P('pts'), may hold values from 0 to 16383, as said below
- owners: int32 [65536], P('pts'), may hold values from 0 to 127, as said below
- conv_weight: bfloat16 [27, 256], replicated, may hold values from -1.5 to 1.5
- norm_gain: float32 [256], replicated, may hold values from 0.1 to 1.9
- norm_bias: float32 [256], replicated, may hold values from -3 to 3
- qkv_weight: bfloat16 [3, 256, 256], P(None, None, 'ch'), may hold values from -20 to 20
- proj_weight: bfloat16 [256, 256], replicated, may hold values from -1.5 to 1.5
- pool_weight: bfloat16 [256, 512], P(None, 'ch'), may hold values from -0.375 to 0.375
Outputs:
- block_out: bfloat16 [65536, 256], P('pts', 'ch')
- pooled: bfloat16 [16384, 512], P('pts', 'ch')
Inputs may be any that keep to these rules, and one draw needn't show every extreme that they name: `owners`: each device's points name every owner at most 8 times; in every draw one owner is named exactly 8 times by the points of every device. `cluster_ids`: cluster ids never fall along the points, every cluster holds one or more points, the points of device i belong to clusters i * 128 - 1 .. i * 128 + 127, and only the first 1 to 3 points of a device (none on device 0) lie in cluster i * 128 - 1; some device has exactly 3 such points. `neighbor_offsets`: offsets -128 and 128 both occur.
All inputs are finite; a program needn't handle non-finite values.
Results may differ from a plain program's by a relative error of at most 0.017.
Values may be sent and summed in bfloat16 or wider, within the bound.
No kernel may reach another device: no remote copies, remote signals or barrier semaphores. Data moves between devices by JAX's collectives and lax.ppermute only.
A program may use at most 64 MiB of HBM per device.

v0:
```python
import math
import jax
import jax.numpy as jnp
from jax import lax
from jax.sharding import PartitionSpec as P

HD = 32
PATCH = 1024
G = 128


def padded_2(value, sides, width):
    for axis, dim in sides:
        devices, length = (lax.axis_size(axis), value.shape[dim])
        up = [(i, (i + 1) % devices) for i in range(devices - 1)]
        down = [(j, i) for i, j in up]
        last = lax.slice_in_dim(value, length - width, length, axis=dim)
        initial = lax.slice_in_dim(value, 0, width, axis=dim)
        before = lax.ppermute(last, axis, up)
        after = lax.ppermute(initial, axis, down)
        value = jnp.concatenate([before, value, after], axis=dim)
    return value


def from_behind(value, axis, by):
    devices = lax.axis_size(axis)
    pairs = [(i, i + by) for i in range(devices) if 0 <= i + by < devices]
    return lax.ppermute(value, axis, pairs)


def attend_patches(packed_rows, live_slots, heads_here):
    slot_total = packed_rows.shape[0]
    patch_count = slot_total // PATCH
    head_cols = packed_rows.shape[1] // 3
    head_size = head_cols // heads_here
    score_scale = 1.0 / math.sqrt(head_size)
    patch_cube = packed_rows.reshape(patch_count, PATCH, 3, heads_here, head_size)
    key_alive = live_slots.reshape(patch_count, PATCH)

    def one_patch(operands):
        patch_rows, alive_keys = operands
        queries = patch_rows[:, 0]
        key_rows = patch_rows[:, 1]
        value_rows = patch_rows[:, 2]
        scores = (
            jnp.einsum("qhd,khd->hqk", queries, key_rows, preferred_element_type=jnp.float32)
            * score_scale
        )
        scores = jnp.where(alive_keys[None, None, :], scores, -1e30)
        row_max = jnp.max(scores, axis=-1, keepdims=True)
        exponent = jnp.exp(scores - row_max)
        denominator = jnp.sum(exponent, axis=-1)
        summed = jnp.einsum(
            "hqk,khd->qhd",
            exponent.astype(jnp.bfloat16),
            value_rows,
            preferred_element_type=jnp.float32,
        )
        return (summed / jnp.transpose(denominator)[:, :, None]).astype(jnp.bfloat16)

    attended = lax.map(one_patch, (patch_cube, key_alive))
    return attended.reshape(slot_total, head_cols)


def shards(
    points_in,
    neighbor_offsets,
    kernel_ids,
    cluster_ids,
    owners,
    conv_weight,
    norm_gain,
    norm_bias,
    qkv_weight,
    proj_weight,
    pool_weight,
):
    point_rows = points_in.shape[0]
    feature_count = points_in.shape[1]
    node_count = lax.axis_size("pts")
    my_index = lax.axis_index("pts")
    channel_index = lax.axis_index("ch")
    capacity = 2 * point_rows // node_count
    slot_total = capacity * node_count
    head_cols = qkv_weight.shape[2]
    heads_here = head_cols // HD
    padded = padded_2(points_in, (("pts", 0),), G)
    offsets_base = jnp.arange(point_rows, dtype=jnp.int32) + G
    kind_ids = jnp.arange(conv_weight.shape[0], dtype=jnp.int32)
    conv = jnp.zeros((point_rows, feature_count), jnp.float32)
    for neighbor_slot in range(neighbor_offsets.shape[1]):
        selector = (kernel_ids[:, neighbor_slot][:, None] == kind_ids[None, :]).astype(jnp.bfloat16)
        weights_here = jnp.dot(selector, conv_weight, preferred_element_type=jnp.float32)
        picked = padded[offsets_base + neighbor_offsets[:, neighbor_slot]]
        conv = conv + weights_here * picked.astype(jnp.float32)
    residual_rows = (points_in.astype(jnp.float32) + conv).astype(jnp.bfloat16)
    features = residual_rows.astype(jnp.float32)
    average = jnp.mean(features, axis=1, keepdims=True)
    centered = features - average
    variance = jnp.mean(centered * centered, axis=1, keepdims=True)
    normed_rows = (centered / jnp.sqrt(variance + 1e-05) * norm_gain + norm_bias).astype(
        jnp.bfloat16
    )
    flat_weight = jnp.transpose(qkv_weight, (1, 0, 2)).reshape(feature_count, 3 * head_cols)
    peer_ids = jnp.arange(node_count, dtype=jnp.int32)
    dest_marks = (owners[:, None] == peer_ids[None, :]).astype(jnp.int32)
    earlier_count = jnp.cumsum(dest_marks, axis=0) - dest_marks
    slot_index = jnp.sum(earlier_count * dest_marks, axis=1)
    send_counts = jnp.sum(dest_marks, axis=0).reshape(node_count, 1)
    position = owners * capacity + slot_index
    projected = jnp.dot(normed_rows, flat_weight, preferred_element_type=jnp.float32).astype(
        jnp.bfloat16
    )
    outgoing = (
        jnp.zeros((slot_total, projected.shape[1]), projected.dtype)
        .at[position]
        .set(projected)
        .reshape(node_count, capacity * 3 * head_cols)
    )
    arrived, incoming_counts = (
        lax.all_to_all(outgoing, "pts", split_axis=0, concat_axis=0, tiled=True),
        lax.all_to_all(send_counts, "pts", split_axis=0, concat_axis=0, tiled=True),
    )
    packed_rows = arrived.reshape(slot_total, 3 * head_cols)
    live_slots = (jnp.arange(capacity, dtype=jnp.int32)[None, :] < incoming_counts).reshape(
        slot_total
    )
    attended = attend_patches(packed_rows, live_slots, heads_here)
    returned_rows = lax.all_to_all(
        attended.reshape(node_count, capacity * head_cols),
        "pts",
        split_axis=0,
        concat_axis=0,
        tiled=True,
    )
    returned = returned_rows.reshape(slot_total, head_cols)[position]
    projected_sum = jnp.dot(
        lax.all_gather(returned, "ch", axis=1, tiled=True),
        proj_weight,
        preferred_element_type=jnp.float32,
    )
    full_out = (residual_rows.astype(jnp.float32) + projected_sum).astype(jnp.bfloat16)
    block_out = lax.dynamic_slice_in_dim(full_out, channel_index * head_cols, head_cols, 1)
    lifted_rows = jnp.dot(full_out, pool_weight, preferred_element_type=jnp.float32)
    cluster_count = point_rows // 4
    local_cluster = cluster_ids - my_index * cluster_count + 1
    cluster_sums = jax.ops.segment_sum(lifted_rows, local_cluster, num_segments=cluster_count + 1)
    point_counts = jax.ops.segment_sum(
        jnp.ones((point_rows,), jnp.float32), local_cluster, num_segments=cluster_count + 1
    )
    spill_sum, spill_count = from_behind((cluster_sums[:1], point_counts[:1]), "pts", -1)
    own_sums = cluster_sums[1:].at[cluster_count - 1].add(spill_sum[0])
    own_counts = point_counts[1:].at[cluster_count - 1].add(spill_count[0])
    pooled = jax.nn.gelu(own_sums / own_counts[:, None], approximate=False).astype(jnp.bfloat16)
    return (block_out, pooled)


def solution(mesh):
    return jax.shard_map(
        shards,
        mesh=mesh,
        in_specs=(
            P("pts", None),
            P("pts", None),
            P("pts", None),
            P("pts"),
            P("pts"),
            P(),
            P(),
            P(),
            P(None, None, "ch"),
            P(),
            P(None, "ch"),
        ),
        out_specs=(P("pts", "ch"), P("pts", "ch")),
        check_vma=False,
    )
```

profile of v0, /device:TPU:1, one launch (start us, length us, event | category | flops | bytes accessed | tf_op | source)
XLA Modules:
  0.0 208.8 jit_solution(9440661710691054107)
XLA Ops:
  1.6 4.6 %collective-permute-start = (bf16[128,256]{1,0:T(8,128)(2,1)S(1)}, bf16[128,256]{1,0:T(8,128)(2,1)S(1)}, u32[]{:S(2)}, u32[]{:S(2)}) collective-permute-start(bf16[128,256]{1,0:T(8,128)(2,1)S(1)} %get-tuple-element.46), channel_id=1, source_target_pairs={{0,4},{4,8},{8,12},{12,16},{16,20},{20,24},{24,28},{28,32},{32,36}... | collective-permute-start | bytes 196616 | tf_op jit(solution)/shard_map/ppermute | solution.py:19
  6.2 5.5 %collective-permute-start.1 = (bf16[128,256]{1,0:T(8,128)(2,1)S(1)}, bf16[128,256]{1,0:T(8,128)(2,1)S(1)}, u32[]{:S(2)}, u32[]{:S(2)}) collective-permute-start(bf16[128,256]{1,0:T(8,128)(2,1)S(1)} %get-tuple-element.45), channel_id=1, source_target_pairs={{4,0},{8,4},{12,8},{16,12},{20,16},{24,20},{28,24},{32,28},{36,32}... | collective-permute-start | bytes 196616 | tf_op jit(solution)/shard_map/ppermute | solution.py:20
  14.4 15.8 %all-to-all-start.1 = ((s32[128,1,1]{2,1,0:T(1,128)}), s32[128,1,1]{2,1,0:T(1,128)S(1)}, u32[]{:S(2)}, u32[]{:S(2)}) async-start(s32[128,1,1]{2,1,0:T(1,128)} %copy.107), calls=%async_computation.1 | async-start | bytes 131072 | tf_op jit(solution)/shard_map/all_to_all | solution.py:122
  60.9 2.1 %gather_fusion.14 = bf16[512,256]{1,0:T(8,128)(2,1)S(1)} fusion(bf16[768,256]{1,0:T(8,128)(2,1)S(1)} %constant_dynamic-update-slice_fusion, s32[1024]{0:T(1024)} %get-tuple-element.82), kind=kCustom, calls=%fused_computation.14 | custom fusion | bytes 526336 | tf_op jit(solution)/shard_map/gather | solution.py:94
  63.9 2.2 %gather_fusion.15 = bf16[512,256]{1,0:T(8,128)(2,1)S(1)} fusion(bf16[768,256]{1,0:T(8,128)(2,1)S(1)} %constant_dynamic-update-slice_fusion, s32[1024]{0:T(1024)} %get-tuple-element.81), kind=kCustom, calls=%fused_computation.15 | custom fusion | bytes 526336 | tf_op jit(solution)/shard_map/gather | solution.py:94
  67.0 2.2 %gather_fusion = bf16[512,256]{1,0:T(8,128)(2,1)S(1)} fusion(bf16[768,256]{1,0:T(8,128)(2,1)S(1)} %constant_dynamic-update-slice_fusion, s32[1024]{0:T(1024)} %get-tuple-element.96), kind=kCustom, calls=%fused_computation | custom fusion | bytes 526336 | tf_op jit(solution)/shard_map/gather | solution.py:94
  72.9 1.9 gather_fusion.2
  86.9 2.1 %gather_fusion.7 = bf16[512,256]{1,0:T(8,128)(2,1)S(1)} fusion(bf16[768,256]{1,0:T(8,128)(2,1)S(1)} %constant_dynamic-update-slice_fusion, s32[1024]{0:T(1024)S(1)} %copy-done.7), kind=kCustom, calls=%fused_computation.7 | custom fusion | bytes 526336 | tf_op jit(solution)/shard_map/gather | solution.py:94
  106.0 5.0 %convert_reduce_fusion = (f32[512]{0:T(512)S(1)}, bf16[512,256]{0,1:T(8,128)(2,1)S(1)}) fusion(f32[512,256]{0,1:T(8,128)} %fusion.48, bf16[512,256]{0,1:T(8,128)(2,1)} %copy.101, f32[512,256]{0,1:T(8,128)} %fusion.47, bf16[512,256]{0,1:T(8,128)(2,1)} %copy.100, f32[512,256]{0,1:T(8,128)} %fusion.46, bf16[512,256]{0,1:T(8,128)(2,1)S(1)} %copy.99, ...), kind=kLoop, calls=%fused_computation.34 | loop fusion | flops 6815232 | bytes 13109248 | tf_op jit(solution)/shard_map/reduce_sum | solution.py:98
  111.6 2.5 %scatter_custom_fusion = bf16[1024,192]{1,0:T(8,128)(2,1)S(1)} fusion(s32[512]{0:T(512)S(1)} %copy-done.14, bf16[512,192]{1,0:T(8,128)(2,1)S(1)} %copy.104, bf16[]{:T(256)} %constant.131.clone.1), kind=kCustom, calls=%fused_computation.54 | custom fusion | bytes 393218 | tf_op jit(solution)/shard_map/scatter | solution.py:117
  115.3 3.0 %reduce.7 = bf16[128,1536]{1,0:T(8,128)(2,1)S(1)} reduce(bf16[128,1,1536]{2,1,0:T(2,128)(2,1)S(1)} %all_to_all.24, bf16[]{:T(256)} %broadcast.271), dimensions={1}, to_apply=%all_to_all.24.reduce_sub_computation | reduce | bytes 786434 | tf_op jit(solution)/shard_map/all_to_all | solution.py:121
  119.2 14.1 %all-to-all-start = ((bf16[128,2,768]{2,1,0:T(2,128)(2,1)}), bf16[128,2,768]{2,1,0:T(2,128)(2,1)S(1)}, u32[]{:S(2)}, u32[]{:S(2)}) async-start(bf16[128,2,768]{2,1,0:T(2,128)(2,1)} %reshape.325), calls=%async_computation | async-start | bytes 786432 | tf_op jit(solution)/shard_map/all_to_all | solution.py:121
  133.3 2.4 %reduce.5 = s32[128]{0:T(128)S(1)} reduce(s32[128,1,1]{2,1,0:T(1,128)S(1)} %all-to-all-done.1, s32[]{:T(128)} %constant.129.clone.1), dimensions={1,2}, to_apply=%all_to_all.21.reduce_sub_computation | reduce | bytes 1028 | tf_op jit(solution)/shard_map/all_to_all | solution.py:122
  135.8 15.2 %all-to-all-done = bf16[128,2,768]{2,1,0:T(2,128)(2,1)S(1)} async-done(((bf16[128,2,768]{2,1,0:T(2,128)(2,1)}), bf16[128,2,768]{2,1,0:T(2,128)(2,1)S(1)}, u32[]{:S(2)}, u32[]{:S(2)}) %all-to-all-start) | async-done | bytes 393248 | tf_op jit(solution)/shard_map/all_to_all | solution.py:121
  151.3 2.4 %reduce.4 = bf16[128,1536]{1,0:T(8,128)(2,1)S(1)} reduce(bf16[128,1,1536]{2,1,0:T(2,128)(2,1)S(1)} %reshape.326, bf16[]{:T(256)} %constant.176), dimensions={1}, to_apply=%all_to_all.19.reduce_sub_computation | reduce | bytes 786434 | tf_op jit(solution)/shard_map/all_to_all | solution.py:121
  158.6 2.4 %fusion.1 = f32[2,1024]{1,0:T(2,128)S(1)} fusion(f32[2,1024,1024]{1,2,0:T(8,128)S(1)} %get-tuple-element.80, f32[2,1024]{1,0:T(2,128)S(1)} %get-tuple-element.79, pred[1024]{0:T(1024)(128)(4,1)S(1)} %lt.115), kind=kLoop, calls=%fused_computation.23 | loop fusion | flops 8386560 | bytes 8406016 | tf_op jit(solution)/shard_map/while/body/eval_jaxpr/reduce_sum | solution.py:52
  166.0 5.5 %all-to-all-start.2 = ((bf16[128,2,256]{2,1,0:T(2,128)(2,1)}), bf16[128,2,256]{2,1,0:T(2,128)(2,1)S(1)}, u32[]{:S(2)}, u32[]{:S(2)}) async-start(bf16[128,2,256]{2,1,0:T(2,128)(2,1)} %reshape.327), calls=%async_computation.2 | async-start | bytes 262144 | tf_op jit(solution)/shard_map/all_to_all | solution.py:129
  171.5 4.1 %scatter_custom_fusion.2 = f32[129]{0:T(256)S(1)} fusion(s32[512]{0:T(512)S(1)} %subtract_add_fusion, f32[512]{0:T(512)S(1)} %broadcast.149, f32[]{:T(128)} %constant.134.clone.1), kind=kCustom, calls=%fused_computation.176 | custom fusion | flops 512 | bytes 520 | tf_op jit(solution)/shard_map/scatter-add | solution.py:148
  176.1 2.9 %collective-permute-start.3 = (f32[1]{0:T(128)}, f32[1]{0:T(128)}, u32[]{:S(2)}, u32[]{:S(2)}) collective-permute-start(f32[1]{0:T(128)} %slice.207), channel_id=1, source_target_pairs={{4,0},{8,4},{12,8},{16,12},{20,16},{24,20},{28,24},{32,28},{36,32}... | collective-permute-start | bytes 20 | tf_op jit(solution)/shard_map/ppermute | solution.py:28
  179.1 2.0 collective-permute-done.3
  181.7 2.6 %all-to-all-done.2 = bf16[128,2,256]{2,1,0:T(2,128)(2,1)S(1)} async-done(((bf16[128,2,256]{2,1,0:T(2,128)(2,1)}), bf16[128,2,256]{2,1,0:T(2,128)(2,1)S(1)}, u32[]{:S(2)}, u32[]{:S(2)}) %all-to-all-start.2) | async-done | bytes 131104 | tf_op jit(solution)/shard_map/all_to_all | solution.py:129
  186.8 10.2 %all-gather = bf16[512,256]{0,1:T(8,128)(2,1)S(1)} all-gather(bf16[512,64]{0,1:T(8,128)(2,1)S(1)} %copy.113), channel_id=2, replica_groups=mesh['pts'=128,'ch'=4] {'ch'}, dimensions={1}, use_global_device_ids=true | all-gather | bytes 327680 | tf_op jit(solution)/shard_map/all_gather | solution.py:138
  197.5 3.5 %scatter_custom_fusion.1 = f32[129,128]{1,0:T(8,128)S(1)} fusion(s32[512]{0:T(512)S(1)} %subtract_add_fusion, f32[512,128]{1,0:T(8,128)S(1)} %fusion.89, f32[]{:T(128)} %constant.134.clone.1), kind=kCustom, calls=%fused_computation.130 | custom fusion | flops 65536 | bytes 66052 | tf_op jit(solution)/shard_map/scatter-add | solution.py:147
  201.0 4.7 %collective-permute-start.2 = (f32[1,128]{1,0:T(1,128)S(1)}, f32[1,128]{1,0:T(1,128)S(1)}, u32[]{:S(2)}, u32[]{:S(2)}) collective-permute-start(f32[1,128]{1,0:T(1,128)S(1)} %slice.248), channel_id=1, source_target_pairs={{4,0},{8,4},{12,8},{16,12},{20,16},{24,20},{28,24},{32,28},{36,32}... | collective-permute-start | bytes 1544 | tf_op jit(solution)/shard_map/ppermute | solution.py:28
  (152 shorter events, 88.4 us)
Async XLA Ops:
  0.6 196.4 %copy-start = (bf16[256,256]{1,0:T(8,128)(2,1)S(1)}, bf16[256,256]{1,0:T(8,128)(2,1)}, u32[]{:S(2)}) copy-start(bf16[256,256]{1,0:T(8,128)(2,1)} %param.24) | copy-start | bytes 393220
  0.6 56.0 %copy-start.4 = (s32[512]{0:T(512)S(1)}, s32[512]{0:T(512)}, u32[]{:S(2)}) copy-start(s32[512]{0:T(512)} %param.19) | copy-start | bytes 6148
  0.7 50.2 %copy-start.1 = (bf16[27,256]{1,0:T(8,128)(2,1)S(1)}, bf16[27,256]{1,0:T(8,128)(2,1)}, u32[]{:S(2)}) copy-start(bf16[27,256]{1,0:T(8,128)(2,1)} %param.20) | copy-start | bytes 41476
  1.6 59.2 %collective-permute-start = (bf16[128,256]{1,0:T(8,128)(2,1)S(1)}, bf16[128,256]{1,0:T(8,128)(2,1)S(1)}, u32[]{:S(2)}, u32[]{:S(2)}) collective-permute-start(bf16[128,256]{1,0:T(8,128)(2,1)S(1)} %get-tuple-element.46), channel_id=1, source_target_pairs={{0,4},{4,8},{8,12},{12,16},{16,20},{20,24},{24,28},{28,32},{32,36}... | collective-permute-start | bytes 196616 | tf_op jit(solution)/shard_map/ppermute | solution.py:19
  6.2 54.7 %collective-permute-start.1 = (bf16[128,256]{1,0:T(8,128)(2,1)S(1)}, bf16[128,256]{1,0:T(8,128)(2,1)S(1)}, u32[]{:S(2)}, u32[]{:S(2)}) collective-permute-start(bf16[128,256]{1,0:T(8,128)(2,1)S(1)} %get-tuple-element.45), channel_id=1, source_target_pairs={{4,0},{8,4},{12,8},{16,12},{20,16},{24,20},{28,24},{32,28},{36,32}... | collective-permute-start | bytes 196616 | tf_op jit(solution)/shard_map/ppermute | solution.py:20
  14.4 104.8 %all-to-all-start.1 = ((s32[128,1,1]{2,1,0:T(1,128)}), s32[128,1,1]{2,1,0:T(1,128)S(1)}, u32[]{:S(2)}, u32[]{:S(2)}) async-start(s32[128,1,1]{2,1,0:T(1,128)} %copy.107), calls=%async_computation.1 | async-start | bytes 131072 | tf_op jit(solution)/shard_map/all_to_all | solution.py:122
  32.0 28.8 %copy-start.2 = (bf16[512,256]{1,0:T(8,128)(2,1)S(1)}, bf16[512,256]{1,0:T(8,128)(2,1)}, u32[]{:S(2)}) copy-start(bf16[512,256]{1,0:T(8,128)(2,1)} %param.15) | copy-start | bytes 786436
  60.9 9.2 %copy-start.13 = (s32[1024]{0:T(1024)S(1)}, s32[1024]{0:T(1024)}, u32[]{:S(2)}) copy-start(s32[1024]{0:T(1024)} %get-tuple-element.95) | copy-start | bytes 12292
  60.9 12.0 %copy-start.12 = (s32[1024]{0:T(1024)S(1)}, s32[1024]{0:T(1024)}, u32[]{:S(2)}) copy-start(s32[1024]{0:T(1024)} %get-tuple-element.94) | copy-start | bytes 12292
  60.9 14.8 %copy-start.11 = (s32[1024]{0:T(1024)S(1)}, s32[1024]{0:T(1024)}, u32[]{:S(2)}) copy-start(s32[1024]{0:T(1024)} %get-tuple-element.93) | copy-start | bytes 12292
  60.9 17.5 %copy-start.10 = (s32[1024]{0:T(1024)S(1)}, s32[1024]{0:T(1024)}, u32[]{:S(2)}) copy-start(s32[1024]{0:T(1024)} %get-tuple-element.92) | copy-start | bytes 12292
  63.9 17.4 %copy-start.9 = (s32[1024]{0:T(1024)S(1)}, s32[1024]{0:T(1024)}, u32[]{:S(2)}) copy-start(s32[1024]{0:T(1024)} %get-tuple-element.91) | copy-start | bytes 12292
  67.0 17.1 %copy-start.8 = (s32[1024]{0:T(1024)S(1)}, s32[1024]{0:T(1024)}, u32[]{:S(2)}) copy-start(s32[1024]{0:T(1024)} %get-tuple-element.90) | copy-start | bytes 12292
  70.0 16.8 %copy-start.7 = (s32[1024]{0:T(1024)S(1)}, s32[1024]{0:T(1024)}, u32[]{:S(2)}) copy-start(s32[1024]{0:T(1024)} %get-tuple-element.89) | copy-start | bytes 12292
  72.8 17.0 %copy-start.6 = (s32[1024]{0:T(1024)S(1)}, s32[1024]{0:T(1024)}, u32[]{:S(2)}) copy-start(s32[1024]{0:T(1024)} %get-tuple-element.88) | copy-start | bytes 12292
  75.7 17.0 %copy-start.5 = (s32[1024]{0:T(1024)S(1)}, s32[1024]{0:T(1024)}, u32[]{:S(2)}) copy-start(s32[1024]{0:T(1024)} %get-tuple-element.87) | copy-start | bytes 12292
  103.0 8.1 %copy-start.17 = (f32[256]{0:T(256)S(1)}, f32[256]{0:T(256)}, u32[]{:S(2)}) copy-start(f32[256]{0:T(256)} %param.22) | copy-start | bytes 3076
  103.0 8.1 %copy-start.18 = (f32[256]{0:T(256)S(1)}, f32[256]{0:T(256)}, u32[]{:S(2)}) copy-start(f32[256]{0:T(256)} %param.21) | copy-start | bytes 3076
  119.2 31.8 %all-to-all-start = ((bf16[128,2,768]{2,1,0:T(2,128)(2,1)}), bf16[128,2,768]{2,1,0:T(2,128)(2,1)S(1)}, u32[]{:S(2)}, u32[]{:S(2)}) async-start(bf16[128,2,768]{2,1,0:T(2,128)(2,1)} %reshape.325), calls=%async_computation | async-start | bytes 786432 | tf_op jit(solution)/shard_map/all_to_all | solution.py:121
  161.0 10.5 %copy-start.15 = (s32[512]{0:T(512)S(1)}, s32[512]{0:T(512)}, u32[]{:S(2)}) copy-start(s32[512]{0:T(512)} %param.18) | copy-start | bytes 6148
  161.0 36.3 %copy-start.3 = (bf16[256,128]{1,0:T(8,128)(2,1)S(1)}, bf16[256,128]{1,0:T(8,128)(2,1)}, u32[]{:S(2)}) copy-start(bf16[256,128]{1,0:T(8,128)(2,1)} %param.25) | copy-start | bytes 196612
  166.0 18.3 %all-to-all-start.2 = ((bf16[128,2,256]{2,1,0:T(2,128)(2,1)}), bf16[128,2,256]{2,1,0:T(2,128)(2,1)S(1)}, u32[]{:S(2)}, u32[]{:S(2)}) async-start(bf16[128,2,256]{2,1,0:T(2,128)(2,1)} %reshape.327), calls=%async_computation.2 | async-start | bytes 262144 | tf_op jit(solution)/shard_map/all_to_all | solution.py:129
  176.1 5.0 %collective-permute-start.3 = (f32[1]{0:T(128)}, f32[1]{0:T(128)}, u32[]{:S(2)}, u32[]{:S(2)}) collective-permute-start(f32[1]{0:T(128)} %slice.207), channel_id=1, source_target_pairs={{4,0},{8,4},{12,8},{16,12},{20,16},{24,20},{28,24},{32,28},{36,32}... | collective-permute-start | bytes 20 | tf_op jit(solution)/shard_map/ppermute | solution.py:28
  201.0 6.4 %collective-permute-start.2 = (f32[1,128]{1,0:T(1,128)S(1)}, f32[1,128]{1,0:T(1,128)S(1)}, u32[]{:S(2)}, u32[]{:S(2)}) collective-permute-start(f32[1,128]{1,0:T(1,128)S(1)} %slice.248), channel_id=1, source_target_pairs={{4,0},{8,4},{12,8},{16,12},{20,16},{24,20},{28,24},{32,28},{36,32}... | collective-permute-start | bytes 1544 | tf_op jit(solution)/shard_map/ppermute | solution.py:28
  (2 other events, 11.0 us)
where the time goes:
time: 213 us; the launch traced here: 209 us
  local copies, waits for them, and re-layouts  63.2 us (30%)
  starting transfers between devices  52.9 us (25%)
  other arithmetic  33.1 us (16%)
  matrix products  26.8 us (13%)
  waiting for transfers between devices  20.8 us (10%)
  blocking collectives  10.2 us (5%)
    gather x32, local copies, waits for them, and re-layouts, shards(): picked = padded[offsets_base + neighbor_offsets[:, neighbor_slot]]  44.9 us
    dot_general x16, matrix products, shards(): jnp.dot(selector, conv_weight, preferred_element_type=jnp.float32)  22.3 us
    all_to_all x1, starting transfers between devices, shards(): lax.all_to_all(send_counts, 'pts', split_axis=0, concat_axis=0, tiled=True)  15.8 us
    all_to_all x1, waiting for transfers between devices, shards(): lax.all_to_all(outgoing, 'pts', split_axis=0, concat_axis=0, tiled=True)  15.2 us
    all_to_all x1, starting transfers between devices, shards(): lax.all_to_all(outgoing, 'pts', split_axis=0, concat_axis=0, tiled=True)  14.1 us
    all_gather x1, blocking collectives, shards(): lax.all_gather(returned, 'ch', axis=1, tiled=True)  10.2 us
    ppermute x2, starting transfers between devices, from_behind(): return lax.ppermute(value, axis, pairs)  7.61 us
    ppermute x1, starting transfers between devices, padded_2(): after = lax.ppermute(initial, axis, down)  5.46 us
  transfers between devices with their start and end apart: 7, of which 4 were waited for; matrix products, arithmetic and copies ran while one was open for 47% of the time, Pallas kernels for 0%

commit v1 on v0

--- a/solution.py
+++ b/solution.py
@@ -135,7 +135,9 @@
     )
     returned = returned_rows.reshape(slot_total, head_cols)[position]
     projected_sum = jnp.dot(
-        lax.all_gather(returned, "ch", axis=1, tiled=True),
+        jnp.concatenate(
+            lax.all_to_all(jnp.stack([returned] * lax.axis_size("ch")), "ch", 0, 0), axis=1
+        ),
         proj_weight,
         preferred_element_type=jnp.float32,
     )

time: 213 us -> 229 us (1.075)
  local copies, waits for them, and re-layouts: 63.2 us -> 75.7 us
  waiting for transfers between devices: 20.8 us -> 32.6 us
  blocking collectives: 10.2 us -> 0 us
    gather x32, local copies, waits for them, and re-layouts: 44.9 us -> 55.1 us  [shards(): picked = padded[offsets_base + neighbor_offsets[:, neighbor_slot]]]
    all_to_all x1, waiting for transfers between devices: 2.58 us -> 12.8 us  [shards(): lax.all_to_all(attended.reshape(node_count, capacity * head_cols), 'pts',...]
    all_gather x1 -> x0, blocking collectives: 10.2 us -> none  [shards(): lax.all_gather(returned, 'ch', axis=1, tiled=True)]
    all_to_all x0 -> x1, starting transfers between devices: none -> 4.01 us  [shards(): lax.all_to_all(jnp.stack([returned] * lax.axis_size('ch')), 'ch', 0, 0)]
    ppermute x2, starting transfers between devices: 7.61 us -> 4.49 us  [from_behind(): return lax.ppermute(value, axis, pairs)]
    unnamed x49 -> x51, local copies, waits for them, and re-layouts: 4.92 us -> 5.78 us
  transfers between devices with their start and end apart: 7 -> 8, of which waited for: 4 -> 4; matrix products, arithmetic and copies ran while one was open for 47% -> 49% of each run, Pallas kernels for 0% -> 0%
where the time goes in v1:
time: 229 us; the launch traced here: 224 us
  local copies, waits for them, and re-layouts  75.7 us (33%)
  starting transfers between devices  53.8 us (23%)
  other arithmetic  33.6 us (15%)
  waiting for transfers between devices  32.6 us (14%)
  matrix products  26.7 us (12%)
    gather x32, local copies, waits for them, and re-layouts, shards(): picked = padded[offsets_base + neighbor_offsets[:, neighbor_slot]]  55.1 us
    dot_general x16, matrix products, shards(): jnp.dot(selector, conv_weight, preferred_element_type=jnp.float32)  22.2 us
    all_to_all x1, waiting for transfers between devices, shards(): lax.all_to_all(outgoing, 'pts', split_axis=0, concat_axis=0, tiled=True)  15.2 us
    all_to_all x1, starting transfers between devices, shards(): lax.all_to_all(send_counts, 'pts', split_axis=0, concat_axis=0, tiled=True)  15.2 us
    all_to_all x1, starting transfers between devices, shards(): lax.all_to_all(outgoing, 'pts', split_axis=0, concat_axis=0, tiled=True)  14.1 us
    all_to_all x1, waiting for transfers between devices, shards(): lax.all_to_all(attended.reshape(node_count, capacity * head_cols), 'pts',...  12.8 us
    ppermute x1, starting transfers between devices, padded_2(): after = lax.ppermute(initial, axis, down)  6.06 us
    unnamed x51, local copies, waits for them, and re-layouts  5.78 us
  transfers between devices with their start and end apart: 8, of which 4 were waited for; matrix products, arithmetic and copies ran while one was open for 49% of the time, Pallas kernels for 0%

profile of v1, /device:TPU:1, one launch (start us, length us, event | category | flops | bytes accessed | tf_op | source)
XLA Modules:
  0.0 224.1 jit_solution(16524759333036613918)
XLA Ops:
  2.3 4.6 %collective-permute-start = (bf16[128,256]{1,0:T(8,128)(2,1)}, bf16[128,256]{1,0:T(8,128)(2,1)}, u32[]{:S(2)}, u32[]{:S(2)}) collective-permute-start(bf16[128,256]{1,0:T(8,128)(2,1)} %get-tuple-element.46), channel_id=1, source_target_pairs={{0,4},{4,8},{8,12},{12,16},{16,20},{20,24},{24,28},{28,32},{32,36}... | collective-permute-start | bytes 196616 | tf_op jit(solution)/shard_map/ppermute | solution.py:19
  6.8 6.1 %collective-permute-start.1 = (bf16[128,256]{1,0:T(8,128)(2,1)}, bf16[128,256]{1,0:T(8,128)(2,1)S(1)}, u32[]{:S(2)}, u32[]{:S(2)}) collective-permute-start(bf16[128,256]{1,0:T(8,128)(2,1)} %get-tuple-element.45), channel_id=1, source_target_pairs={{4,0},{8,4},{12,8},{16,12},{20,16},{24,20},{28,24},{32,28},{36,32}... | collective-permute-start | bytes 196616 | tf_op jit(solution)/shard_map/ppermute | solution.py:20
  15.7 15.2 %all-to-all-start.1 = ((s32[128,1,1]{2,1,0:T(1,128)}), s32[128,1,1]{2,1,0:T(1,128)S(1)}, u32[]{:S(2)}, u32[]{:S(2)}) async-start(s32[128,1,1]{2,1,0:T(1,128)} %copy.108), calls=%async_computation.1 | async-start | bytes 131072 | tf_op jit(solution)/shard_map/all_to_all | solution.py:122
  91.8 2.6 %gather_fusion.7 = bf16[512,256]{1,0:T(8,128)(2,1)} fusion(bf16[768,256]{1,0:T(8,128)(2,1)S(1)} %constant_dynamic-update-slice_fusion, s32[1024]{0:T(1024)S(1)} %copy-done.7), kind=kCustom, calls=%fused_computation.7 | custom fusion | bytes 526336 | tf_op jit(solution)/shard_map/gather | solution.py:94
  96.2 2.6 %gather_fusion.8 = bf16[512,256]{1,0:T(8,128)(2,1)} fusion(bf16[768,256]{1,0:T(8,128)(2,1)S(1)} %constant_dynamic-update-slice_fusion, s32[1024]{0:T(1024)S(1)} %copy-done.6), kind=kCustom, calls=%fused_computation.8 | custom fusion | bytes 526336 | tf_op jit(solution)/shard_map/gather | solution.py:94
  100.6 2.6 %gather_fusion.9 = bf16[512,256]{1,0:T(8,128)(2,1)} fusion(bf16[768,256]{1,0:T(8,128)(2,1)S(1)} %constant_dynamic-update-slice_fusion, s32[1024]{0:T(1024)S(1)} %get-tuple-element.87), kind=kCustom, calls=%fused_computation.9 | custom fusion | bytes 526336 | tf_op jit(solution)/shard_map/gather | solution.py:94
  105.0 2.6 %gather_fusion.10 = bf16[512,256]{1,0:T(8,128)(2,1)} fusion(bf16[768,256]{1,0:T(8,128)(2,1)S(1)} %constant_dynamic-update-slice_fusion, s32[1024]{0:T(1024)S(1)} %get-tuple-element.86), kind=kCustom, calls=%fused_computation.10 | custom fusion | bytes 526336 | tf_op jit(solution)/shard_map/gather | solution.py:94
  109.3 2.6 %gather_fusion.11 = bf16[512,256]{1,0:T(8,128)(2,1)} fusion(bf16[768,256]{1,0:T(8,128)(2,1)S(1)} %constant_dynamic-update-slice_fusion, s32[1024]{0:T(1024)S(1)} %get-tuple-element.85), kind=kCustom, calls=%fused_computation.11 | custom fusion | bytes 526336 | tf_op jit(solution)/shard_map/gather | solution.py:94
  113.7 2.6 %gather_fusion.12 = bf16[512,256]{1,0:T(8,128)(2,1)} fusion(bf16[768,256]{1,0:T(8,128)(2,1)S(1)} %constant_dynamic-update-slice_fusion, s32[1024]{0:T(1024)S(1)} %get-tuple-element.84), kind=kCustom, calls=%fused_computation.12 | custom fusion | bytes 526336 | tf_op jit(solution)/shard_map/gather | solution.py:94
  118.1 4.9 %convert_reduce_fusion = (f32[512]{0:T(512)S(1)}, bf16[512,256]{0,1:T(8,128)(2,1)S(1)}) fusion(f32[512,256]{0,1:T(8,128)} %fusion.48, bf16[512,256]{0,1:T(8,128)(2,1)} %copy.102, f32[512,256]{0,1:T(8,128)} %fusion.47, bf16[512,256]{0,1:T(8,128)(2,1)} %copy.101, f32[512,256]{0,1:T(8,128)} %fusion.46, bf16[512,256]{0,1:T(8,128)(2,1)} %copy.100, ...), kind=kLoop, calls=%fused_computation.34 | loop fusion | flops 6815232 | bytes 13109248 | tf_op jit(solution)/shard_map/reduce_sum | solution.py:98
  123.7 2.5 %scatter_custom_fusion = bf16[1024,192]{1,0:T(8,128)(2,1)S(1)} fusion(s32[512]{0:T(512)S(1)} %copy-done.15, bf16[512,192]{1,0:T(8,128)(2,1)S(1)} %copy.105, bf16[]{:T(256)} %constant.131.clone.1), kind=kCustom, calls=%fused_computation.54 | custom fusion | bytes 393218 | tf_op jit(solution)/shard_map/scatter | solution.py:117
  127.4 3.0 %reduce.7 = bf16[128,1536]{1,0:T(8,128)(2,1)S(1)} reduce(bf16[128,1,1536]{2,1,0:T(2,128)(2,1)S(1)} %all_to_all.28, bf16[]{:T(256)} %broadcast.273), dimensions={1}, to_apply=%all_to_all.28.reduce_sub_computation | reduce | bytes 786434 | tf_op jit(solution)/shard_map/all_to_all | solution.py:121
  131.2 14.1 %all-to-all-start = ((bf16[128,2,768]{2,1,0:T(2,128)(2,1)}), bf16[128,2,768]{2,1,0:T(2,128)(2,1)S(1)}, u32[]{:S(2)}, u32[]{:S(2)}) async-start(bf16[128,2,768]{2,1,0:T(2,128)(2,1)} %reshape.334), calls=%async_computation | async-start | bytes 786432 | tf_op jit(solution)/shard_map/all_to_all | solution.py:121
  145.3 2.4 %reduce.5 = s32[128]{0:T(128)S(1)} reduce(s32[128,1,1]{2,1,0:T(1,128)S(1)} %all-to-all-done.1, s32[]{:T(128)} %constant.129.clone.1), dimensions={1,2}, to_apply=%all_to_all.24.reduce_sub_computation | reduce | bytes 1028 | tf_op jit(solution)/shard_map/all_to_all | solution.py:122
  147.9 15.2 %all-to-all-done = bf16[128,2,768]{2,1,0:T(2,128)(2,1)S(1)} async-done(((bf16[128,2,768]{2,1,0:T(2,128)(2,1)}), bf16[128,2,768]{2,1,0:T(2,128)(2,1)S(1)}, u32[]{:S(2)}, u32[]{:S(2)}) %all-to-all-start) | async-done | bytes 393248 | tf_op jit(solution)/shard_map/all_to_all | solution.py:121
  163.4 2.4 %reduce.4 = bf16[128,1536]{1,0:T(8,128)(2,1)S(1)} reduce(bf16[128,1,1536]{2,1,0:T(2,128)(2,1)S(1)} %reshape.335, bf16[]{:T(256)} %constant.176), dimensions={1}, to_apply=%all_to_all.22.reduce_sub_computation | reduce | bytes 786434 | tf_op jit(solution)/shard_map/all_to_all | solution.py:121
  170.6 2.4 %fusion.1 = f32[2,1024]{1,0:T(2,128)S(1)} fusion(f32[2,1024,1024]{1,2,0:T(8,128)S(1)} %get-tuple-element.80, f32[2,1024]{1,0:T(2,128)S(1)} %get-tuple-element.79, pred[1024]{0:T(1024)(128)(4,1)S(1)} %lt.115), kind=kLoop, calls=%fused_computation.23 | loop fusion | flops 8386560 | bytes 8406016 | tf_op jit(solution)/shard_map/while/body/eval_jaxpr/reduce_sum | solution.py:52
  178.1 5.4 %all-to-all-start.2 = ((bf16[128,2,256]{2,1,0:T(2,128)(2,1)}), bf16[128,2,256]{2,1,0:T(2,128)(2,1)S(1)}, u32[]{:S(2)}, u32[]{:S(2)}) async-start(bf16[128,2,256]{2,1,0:T(2,128)(2,1)} %reshape.336), calls=%async_computation.2 | async-start | bytes 262144 | tf_op jit(solution)/shard_map/all_to_all | solution.py:129
  183.5 12.8 %all-to-all-done.2 = bf16[128,2,256]{2,1,0:T(2,128)(2,1)S(1)} async-done(((bf16[128,2,256]{2,1,0:T(2,128)(2,1)}), bf16[128,2,256]{2,1,0:T(2,128)(2,1)S(1)}, u32[]{:S(2)}, u32[]{:S(2)}) %all-to-all-start.2) | async-done | bytes 131104 | tf_op jit(solution)/shard_map/all_to_all | solution.py:129
  199.5 4.0 %all-to-all-start.3 = ((bf16[4,512,64]{1,2,0:T(8,128)(2,1)}), bf16[4,512,64]{1,2,0:T(8,128)(2,1)S(1)}, u32[]{:S(2)}, u32[]{:S(2)}) async-start(bf16[4,512,64]{1,2,0:T(8,128)(2,1)} %stack.2), calls=%async_computation.3 | async-start | bytes 524288 | tf_op jit(solution)/shard_map/all_to_all | solution.py:139
  203.6 4.1 %scatter_custom_fusion.2 = f32[129]{0:T(256)S(1)} fusion(s32[512]{0:T(512)S(1)} %subtract_add_fusion, f32[512]{0:T(512)S(1)} %broadcast.151, f32[]{:T(128)} %constant.134.clone.1), kind=kCustom, calls=%fused_computation.176 | custom fusion | flops 512 | bytes 520 | tf_op jit(solution)/shard_map/scatter-add | solution.py:150
  208.2 2.6 %collective-permute-start.3 = (f32[1]{0:T(128)}, f32[1]{0:T(128)}, u32[]{:S(2)}, u32[]{:S(2)}) collective-permute-start(f32[1]{0:T(128)} %slice.207), channel_id=1, source_target_pairs={{4,0},{8,4},{12,8},{16,12},{20,16},{24,20},{28,24},{32,28},{36,32}... | collective-permute-start | bytes 20 | tf_op jit(solution)/shard_map/ppermute | solution.py:28
  210.8 2.3 %collective-permute-done.3 = f32[1]{0:T(128)} collective-permute-done((f32[1]{0:T(128)}, f32[1]{0:T(128)}, u32[]{:S(2)}, u32[]{:S(2)}) %collective-permute-start.3) | collective-permute-done | bytes 36 | tf_op jit(solution)/shard_map/ppermute | solution.py:28
  214.4 3.5 %scatter_custom_fusion.1 = f32[129,128]{1,0:T(8,128)S(1)} fusion(s32[512]{0:T(512)S(1)} %subtract_add_fusion, f32[512,128]{1,0:T(8,128)S(1)} %fusion.89, f32[]{:T(128)} %constant.134.clone.1), kind=kCustom, calls=%fused_computation.130 | custom fusion | flops 65536 | bytes 66052 | tf_op jit(solution)/shard_map/scatter-add | solution.py:149
  (156 shorter events, 99.7 us)
Async XLA Ops:
  0.6 213.2 %copy-start = (bf16[256,256]{1,0:T(8,128)(2,1)S(1)}, bf16[256,256]{1,0:T(8,128)(2,1)}, u32[]{:S(2)}) copy-start(bf16[256,256]{1,0:T(8,128)(2,1)} %param.24) | copy-start | bytes 393220
  0.6 62.1 %copy-start.2 = (bf16[512,256]{1,0:T(8,128)(2,1)S(1)}, bf16[512,256]{1,0:T(8,128)(2,1)}, u32[]{:S(2)}) copy-start(bf16[512,256]{1,0:T(8,128)(2,1)} %param.15) | copy-start | bytes 786436
  0.7 56.5 %copy-start.5 = (s32[512]{0:T(512)S(1)}, s32[512]{0:T(512)}, u32[]{:S(2)}) copy-start(s32[512]{0:T(512)} %param.19) | copy-start | bytes 6148
  0.7 50.7 %copy-start.1 = (bf16[27,256]{1,0:T(8,128)(2,1)S(1)}, bf16[27,256]{1,0:T(8,128)(2,1)}, u32[]{:S(2)}) copy-start(bf16[27,256]{1,0:T(8,128)(2,1)} %param.20) | copy-start | bytes 41476
  2.3 59.6 %collective-permute-start = (bf16[128,256]{1,0:T(8,128)(2,1)}, bf16[128,256]{1,0:T(8,128)(2,1)}, u32[]{:S(2)}, u32[]{:S(2)}) collective-permute-start(bf16[128,256]{1,0:T(8,128)(2,1)} %get-tuple-element.46), channel_id=1, source_target_pairs={{0,4},{4,8},{8,12},{12,16},{16,20},{20,24},{24,28},{28,32},{32,36}... | collective-permute-start | bytes 196616 | tf_op jit(solution)/shard_map/ppermute | solution.py:19
  6.8 55.9 %collective-permute-start.1 = (bf16[128,256]{1,0:T(8,128)(2,1)}, bf16[128,256]{1,0:T(8,128)(2,1)S(1)}, u32[]{:S(2)}, u32[]{:S(2)}) collective-permute-start(bf16[128,256]{1,0:T(8,128)(2,1)} %get-tuple-element.45), channel_id=1, source_target_pairs={{4,0},{8,4},{12,8},{16,12},{20,16},{24,20},{28,24},{32,28},{36,32}... | collective-permute-start | bytes 196616 | tf_op jit(solution)/shard_map/ppermute | solution.py:20
  15.7 115.6 %all-to-all-start.1 = ((s32[128,1,1]{2,1,0:T(1,128)}), s32[128,1,1]{2,1,0:T(1,128)S(1)}, u32[]{:S(2)}, u32[]{:S(2)}) async-start(s32[128,1,1]{2,1,0:T(1,128)} %copy.108), calls=%async_computation.1 | async-start | bytes 131072 | tf_op jit(solution)/shard_map/all_to_all | solution.py:122
  62.8 12.0 %copy-start.13 = (s32[1024]{0:T(1024)S(1)}, s32[1024]{0:T(1024)}, u32[]{:S(2)}) copy-start(s32[1024]{0:T(1024)} %get-tuple-element.95) | copy-start | bytes 12292
  62.8 14.8 %copy-start.12 = (s32[1024]{0:T(1024)S(1)}, s32[1024]{0:T(1024)}, u32[]{:S(2)}) copy-start(s32[1024]{0:T(1024)} %get-tuple-element.94) | copy-start | bytes 12292
  62.8 17.6 %copy-start.11 = (s32[1024]{0:T(1024)S(1)}, s32[1024]{0:T(1024)}, u32[]{:S(2)}) copy-start(s32[1024]{0:T(1024)} %get-tuple-element.93) | copy-start | bytes 12292
  65.8 17.4 %copy-start.10 = (s32[1024]{0:T(1024)S(1)}, s32[1024]{0:T(1024)}, u32[]{:S(2)}) copy-start(s32[1024]{0:T(1024)} %get-tuple-element.92) | copy-start | bytes 12292
  68.9 17.1 %copy-start.9 = (s32[1024]{0:T(1024)S(1)}, s32[1024]{0:T(1024)}, u32[]{:S(2)}) copy-start(s32[1024]{0:T(1024)} %get-tuple-element.91) | copy-start | bytes 12292
  72.0 16.9 %copy-start.8 = (s32[1024]{0:T(1024)S(1)}, s32[1024]{0:T(1024)}, u32[]{:S(2)}) copy-start(s32[1024]{0:T(1024)} %get-tuple-element.90) | copy-start | bytes 12292
  74.8 17.0 %copy-start.7 = (s32[1024]{0:T(1024)S(1)}, s32[1024]{0:T(1024)}, u32[]{:S(2)}) copy-start(s32[1024]{0:T(1024)} %get-tuple-element.89) | copy-start | bytes 12292
  77.6 18.6 %copy-start.6 = (s32[1024]{0:T(1024)S(1)}, s32[1024]{0:T(1024)}, u32[]{:S(2)}) copy-start(s32[1024]{0:T(1024)} %get-tuple-element.88) | copy-start | bytes 12292
  91.8 26.3 %copy-start.3 = (bf16[512,256]{0,1:T(8,128)(2,1)S(1)}, bf16[512,256]{0,1:T(8,128)(2,1)}, u32[]{:S(2)}) copy-start(bf16[512,256]{0,1:T(8,128)(2,1)} %copy.86) | copy-start | bytes 786436
  111.9 11.3 %copy-start.19 = (f32[256]{0:T(256)S(1)}, f32[256]{0:T(256)}, u32[]{:S(2)}) copy-start(f32[256]{0:T(256)} %param.21) | copy-start | bytes 3076
  131.2 31.8 %all-to-all-start = ((bf16[128,2,768]{2,1,0:T(2,128)(2,1)}), bf16[128,2,768]{2,1,0:T(2,128)(2,1)S(1)}, u32[]{:S(2)}, u32[]{:S(2)}) async-start(bf16[128,2,768]{2,1,0:T(2,128)(2,1)} %reshape.334), calls=%async_computation | async-start | bytes 786432 | tf_op jit(solution)/shard_map/all_to_all | solution.py:121
  173.0 30.5 %copy-start.16 = (s32[512]{0:T(512)S(1)}, s32[512]{0:T(512)}, u32[]{:S(2)}) copy-start(s32[512]{0:T(512)} %param.18) | copy-start | bytes 6148
  173.1 41.1 %copy-start.4 = (bf16[256,128]{1,0:T(8,128)(2,1)S(1)}, bf16[256,128]{1,0:T(8,128)(2,1)}, u32[]{:S(2)}) copy-start(bf16[256,128]{1,0:T(8,128)(2,1)} %param.25) | copy-start | bytes 196612
  178.1 18.3 %all-to-all-start.2 = ((bf16[128,2,256]{2,1,0:T(2,128)(2,1)}), bf16[128,2,256]{2,1,0:T(2,128)(2,1)S(1)}, u32[]{:S(2)}, u32[]{:S(2)}) async-start(bf16[128,2,256]{2,1,0:T(2,128)(2,1)} %reshape.336), calls=%async_computation.2 | async-start | bytes 262144 | tf_op jit(solution)/shard_map/all_to_all | solution.py:129
  199.5 14.3 %all-to-all-start.3 = ((bf16[4,512,64]{1,2,0:T(8,128)(2,1)}), bf16[4,512,64]{1,2,0:T(8,128)(2,1)S(1)}, u32[]{:S(2)}, u32[]{:S(2)}) async-start(bf16[4,512,64]{1,2,0:T(8,128)(2,1)} %stack.2), calls=%async_computation.3 | async-start | bytes 524288 | tf_op jit(solution)/shard_map/all_to_all | solution.py:139
  208.2 5.0 %collective-permute-start.3 = (f32[1]{0:T(128)}, f32[1]{0:T(128)}, u32[]{:S(2)}, u32[]{:S(2)}) collective-permute-start(f32[1]{0:T(128)} %slice.207), channel_id=1, source_target_pairs={{4,0},{8,4},{12,8},{16,12},{20,16},{24,20},{28,24},{32,28},{36,32}... | collective-permute-start | bytes 20 | tf_op jit(solution)/shard_map/ppermute | solution.py:28
  217.9 4.9 %collective-permute-start.2 = (f32[1,128]{1,0:T(1,128)S(1)}, f32[1,128]{1,0:T(1,128)S(1)}, u32[]{:S(2)}, u32[]{:S(2)}) collective-permute-start(f32[1,128]{1,0:T(1,128)S(1)} %slice.248), channel_id=1, source_target_pairs={{4,0},{8,4},{12,8},{16,12},{20,16},{24,20},{28,24},{32,28},{36,32}... | collective-permute-start | bytes 1544 | tf_op jit(solution)/shard_map/ppermute | solution.py:28
  (4 other events, 32.9 us)
